TPU v7x, 32 devices: a whole 2x2x4 slice. The times are simulated.
32 devices in a mesh: fsdp: 8 (over y, x, core), tp: 4 (over z).
Axes of the slice: x: 2, y: 2, z: 4, core: 2. Of those that a mesh axis runs over, the one named last changes fastest.
Arguments:
- layer_input: bfloat16 [24576, 512], P(('fsdp', 'tp')), may hold values from -6 to 6
- segment_ids: int32 [24, 1024], P('fsdp'), may hold values from 0 to 15, never falling along the last dimension, each value on 1 to 512 neighbouring positions
- valid_mask: int32 [24576], P(('fsdp', 'tp')), may hold values from 0 to 1, as said below
- teacher: bfloat16 [24576, 512], P(('fsdp', 'tp')), may hold values from -6 to 6
- cotangent: bfloat16 [24576, 512], P(('fsdp', 'tp')), may hold values from -6 to 6
- ln1_gain: bfloat16 [512], P('fsdp'), may hold values from 0.099609375 to 1.8984375
- ln1_bias: bfloat16 [512], P('fsdp'), may hold values from -1.75 to 1.75
- w_q: bfloat16 [512, 512], P('fsdp', 'tp'), may hold values from -0.25 to 0.25
- w_k: bfloat16 [512, 512], P('fsdp', 'tp'), may hold values from -0.25 to 0.25
- w_v: bfloat16 [512, 512], P('fsdp', 'tp'), may hold values from -0.25 to 0.25
- b_q: bfloat16 [8, 64], P('tp', 'fsdp'), may hold values from -3 to 3
- b_v: bfloat16 [8, 64], P('tp', 'fsdp'), may hold values from -3 to 3
- w_o: bfloat16 [512, 512], P('tp', 'fsdp'), may hold values from -1 to 1
- b_o: bfloat16 [512], P('fsdp'), may hold values from -3 to 3
- ln2_gain: bfloat16 [512], P('fsdp'), may hold values from 0.099609375 to 1.8984375
- ln2_bias: bfloat16 [512], P('fsdp'), may hold values from -1.75 to 1.75
- w_up: bfloat16 [512, 2048], P('fsdp', 'tp'), may hold values from -0.25 to 0.25
- b_up: bfloat16 [32, 64], P('tp', 'fsdp'), may hold values from -3 to 3
- w_down: bfloat16 [2048, 512], P('tp', 'fsdp'), may hold values from -0.25 to 0.25
- b_down: bfloat16 [512], P('fsdp'), may hold values from -3 to 3
Outputs:
- layer_out: bfloat16 [24576, 512], P(('fsdp', 'tp'))
- loss: float32 [], replicated
- grad_layer_input: float32 [24576, 512], P(('fsdp', 'tp'))
- grad_ln1_gain: float32 [512], P('fsdp')
- grad_ln1_bias: float32 [512], P('fsdp')
- grad_w_q: float32 [512, 512], P('fsdp', 'tp')
- grad_w_k: float32 [512, 512], P('fsdp', 'tp')
- grad_w_v: float32 [512, 512], P('fsdp', 'tp')
- grad_b_q: float32 [8, 64], P('tp', 'fsdp')
- grad_b_v: float32 [8, 64], P('tp', 'fsdp')
- grad_w_o: float32 [512, 512], P('tp', 'fsdp')
- grad_b_o: float32 [512], P('fsdp')
- grad_ln2_gain: float32 [512], P('fsdp')
- grad_ln2_bias: float32 [512], P('fsdp')
- grad_w_up: float32 [512, 2048], P('fsdp', 'tp')
- grad_b_up: float32 [32, 64], P('tp', 'fsdp')
- grad_w_down: float32 [2048, 512], P('tp', 'fsdp')
- grad_b_down: float32 [512], P('fsdp')
Inputs may be any that keep to these rules, and one draw needn't show every extreme that they name: `segment_ids`: in each sequence the ids never fall, each document holds 1 to 512 positions, and one holds exactly 512. `valid_mask`: the first token of every sequence is 1.
All inputs are finite; a program needn't handle non-finite values.
Results may differ from a plain program's by a relative error of at most 0.014.
Values may be sent and summed in bfloat16 or wider, within the bound.
No kernel may reach another device: no remote copies, remote signals or barrier semaphores. Data moves between devices by JAX's collectives and lax.ppermute only.
A program may use at most 128 MiB of HBM per device.

v0:
```python
import jax
import jax.numpy as jnp
from jax import lax
from jax.sharding import PartitionSpec as P

D = 512
HD = 64
LEN = 1024


def layer_norm(values, gains, offsets):
    center = values - jnp.mean(values, axis=-1, keepdims=True)
    spread = jnp.mean(center * center, axis=-1, keepdims=True)
    return center * lax.rsqrt(spread + 1e-05) * gains + offsets


def quick_gelu(values):
    return values * jax.nn.sigmoid(1.702 * values)


def block_scores(query_block, key_seq, segment_seq, first_row):
    block_rows = query_block.shape[0]
    query_place = first_row + jnp.arange(block_rows, dtype=jnp.int32)
    key_place = jnp.arange(key_seq.shape[0], dtype=jnp.int32)
    query_segment = lax.dynamic_slice_in_dim(segment_seq, first_row, block_rows)
    allowed = (query_segment[:, None] == segment_seq[None, :]) & (
        key_place[None, :] <= query_place[:, None]
    )
    raw_scores = jnp.einsum(
        "qhd,khd->hqk", query_block, key_seq, preferred_element_type=jnp.float32
    ) * HD ** (-0.5)
    return jnp.where(allowed[None], raw_scores, -1e30)


def forward_sequence(inputs):
    query_seq, key_seq, value_seq, segment_seq = inputs

    def forward_one_block(element):
        block_index, query_block = element
        scores = block_scores(query_block, key_seq, segment_seq, block_index * query_block.shape[0])
        row_max = jnp.max(scores, axis=-1, keepdims=True)
        exponent = jnp.exp(scores - row_max)
        row_sum = jnp.sum(exponent, axis=-1, keepdims=True)
        weights = (exponent / row_sum).astype(jnp.bfloat16)
        attended = jnp.einsum(
            "hqk,khd->qhd", weights, value_seq, preferred_element_type=jnp.float32
        )
        return (attended.astype(jnp.bfloat16), (row_max + jnp.log(row_sum))[..., 0])

    return lax.map(forward_one_block, (jnp.arange(query_seq.shape[0], dtype=jnp.int32), query_seq))


def backward_sequence(inputs):
    query_seq, key_seq, value_seq, segment_seq, total_seq, grad_out_seq = inputs
    zero_grads = jnp.zeros(key_seq.shape, jnp.float32)

    def backward_one_block(carried, element):
        grad_keys, grad_values = carried
        block_index, query_block, total_block, grad_block = element
        scores = block_scores(query_block, key_seq, segment_seq, block_index * query_block.shape[0])
        weights = jnp.exp(scores - total_block[..., None])
        grad_values = grad_values + jnp.einsum(
            "hqk,qhd->khd",
            weights.astype(jnp.bfloat16),
            grad_block,
            preferred_element_type=jnp.float32,
        )
        grad_weights = jnp.einsum(
            "qhd,khd->hqk", grad_block, value_seq, preferred_element_type=jnp.float32
        )
        grad_scores = (
            weights * (grad_weights - jnp.sum(weights * grad_weights, axis=-1, keepdims=True))
        ).astype(jnp.bfloat16)
        grad_query = jnp.einsum(
            "hqk,khd->qhd", grad_scores, key_seq, preferred_element_type=jnp.float32
        ) * HD ** (-0.5)
        grad_keys = grad_keys + jnp.einsum(
            "hqk,qhd->khd", grad_scores, query_block, preferred_element_type=jnp.float32
        ) * HD ** (-0.5)
        return ((grad_keys, grad_values), grad_query.astype(jnp.bfloat16))

    (grad_keys, grad_values), grad_queries = lax.scan(
        backward_one_block,
        (zero_grads, zero_grads),
        (jnp.arange(query_seq.shape[0], dtype=jnp.int32), query_seq, total_seq, grad_out_seq),
    )
    return (grad_queries, grad_keys.astype(jnp.bfloat16), grad_values.astype(jnp.bfloat16))


def local(
    layer_input,
    segment_ids,
    valid_mask,
    teacher,
    cotangent,
    ln1_gain,
    ln1_bias,
    w_q,
    w_k,
    w_v,
    b_q,
    b_v,
    w_o,
    b_o,
    ln2_gain,
    ln2_bias,
    w_up,
    b_up,
    w_down,
    b_down,
):
    fsdp_size = lax.axis_size("fsdp")
    tensor_size = lax.axis_size("tp")
    local_rows = layer_input.shape[0]
    (
        gain_one,
        bias_one,
        query_w,
        key_w,
        value_w,
        query_b,
        value_b,
        out_w,
        out_b,
        gain_two,
        bias_two,
        upper_w,
        upper_b,
        lower_w,
        lower_b,
    ) = (
        lax.all_gather(ln1_gain, "fsdp", axis=0, tiled=True),
        lax.all_gather(ln1_bias, "fsdp", axis=0, tiled=True),
        lax.all_gather(w_q, "fsdp", axis=0, tiled=True),
        lax.all_gather(w_k, "fsdp", axis=0, tiled=True),
        lax.all_gather(w_v, "fsdp", axis=0, tiled=True),
        lax.all_gather(b_q, "fsdp", axis=1, tiled=True),
        lax.all_gather(b_v, "fsdp", axis=1, tiled=True),
        lax.all_gather(w_o, "fsdp", axis=1, tiled=True),
        lax.all_gather(b_o, "fsdp", axis=0, tiled=True),
        lax.all_gather(ln2_gain, "fsdp", axis=0, tiled=True),
        lax.all_gather(ln2_bias, "fsdp", axis=0, tiled=True),
        lax.all_gather(w_up, "fsdp", axis=0, tiled=True),
        lax.all_gather(b_up, "fsdp", axis=1, tiled=True),
        lax.all_gather(w_down, "fsdp", axis=1, tiled=True),
        lax.all_gather(b_down, "fsdp", axis=0, tiled=True),
    )
    mask_float = valid_mask.astype(jnp.float32)
    valid_total = lax.psum(jnp.sum(mask_float), ("fsdp", "tp"))
    tokens_all = local_rows * fsdp_size * tensor_size
    input_float = layer_input.astype(jnp.float32)
    gain_first = gain_one.astype(jnp.float32)
    bias_first = bias_one.astype(jnp.float32)
    gain_second = gain_two.astype(jnp.float32)
    bias_second = bias_two.astype(jnp.float32)
    normed_one = layer_norm(input_float, gain_first, bias_first).astype(jnp.bfloat16)
    head_count = query_w.shape[1] // HD
    rows_one = lax.all_gather(normed_one, "tp", axis=0, tiled=True)
    queries = (
        jnp.dot(rows_one, query_w, preferred_element_type=jnp.float32)
        + query_b.reshape(-1).astype(jnp.float32)
    ).astype(jnp.bfloat16)
    keys_all = jnp.dot(rows_one, key_w, preferred_element_type=jnp.float32).astype(jnp.bfloat16)
    values_all = (
        jnp.dot(rows_one, value_w, preferred_element_type=jnp.float32)
        + value_b.reshape(-1).astype(jnp.float32)
    ).astype(jnp.bfloat16)
    seq_count = segment_ids.shape[0]
    block_rows = min(512, LEN)
    block_count = LEN // block_rows
    shaped_queries = queries.reshape(seq_count, block_count, block_rows, head_count, HD)
    shaped_keys = keys_all.reshape(seq_count, LEN, head_count, HD)
    shaped_values = values_all.reshape(seq_count, LEN, head_count, HD)
    attended, log_totals = lax.map(
        forward_sequence, (shaped_queries, shaped_keys, shaped_values, segment_ids)
    )
    attended = attended.reshape(-1, head_count * HD)
    attention = lax.psum_scatter(
        jnp.dot(attended, out_w, preferred_element_type=jnp.float32).astype(jnp.bfloat16),
        "tp",
        scatter_dimension=0,
        tiled=True,
    ).astype(jnp.float32)
    hidden_one = input_float + attention + out_b.astype(jnp.float32)
    normed_two = layer_norm(hidden_one, gain_second, bias_second).astype(jnp.bfloat16)
    rows_two = lax.all_gather(normed_two, "tp", axis=0, tiled=True)
    pre_act = jnp.dot(rows_two, upper_w, preferred_element_type=jnp.float32) + upper_b.reshape(
        -1
    ).astype(jnp.float32)
    activated = quick_gelu(pre_act).astype(jnp.bfloat16)
    branch = lax.psum_scatter(
        jnp.dot(activated, lower_w, preferred_element_type=jnp.float32).astype(jnp.bfloat16),
        "tp",
        scatter_dimension=0,
        tiled=True,
    ).astype(jnp.float32)
    out_full = hidden_one + branch + lower_b.astype(jnp.float32)
    difference = out_full - teacher.astype(jnp.float32)
    square_part = jnp.sum(mask_float * jnp.mean(difference * difference, axis=-1))
    grad_out = (
        cotangent.astype(jnp.float32) + tokens_all / valid_total * mask_float[:, None] * difference
    )
    grad_lower_bias = jnp.sum(grad_out, axis=0)
    grad_out_low = grad_out.astype(jnp.bfloat16)
    grad_rows = lax.all_gather(grad_out_low, "tp", axis=0, tiled=True)
    grad_hidden_units = jnp.einsum(
        "nd,fd->nf", grad_rows, lower_w, preferred_element_type=jnp.float32
    )
    grad_lower = jnp.einsum("nf,nd->fd", activated, grad_rows, preferred_element_type=jnp.float32)
    gelu_value, gelu_pull = jax.vjp(quick_gelu, pre_act)
    grad_pre = gelu_pull(grad_hidden_units)[0].astype(jnp.bfloat16)
    grad_upper = jnp.einsum("nd,nf->df", rows_two, grad_pre, preferred_element_type=jnp.float32)
    grad_upper_bias = jnp.sum(grad_pre, axis=0, dtype=jnp.float32).reshape(upper_b.shape)
    grad_normed_two = lax.psum_scatter(
        jnp.einsum("nf,df->nd", grad_pre, upper_w, preferred_element_type=jnp.float32).astype(
            jnp.bfloat16
        ),
        "tp",
        scatter_dimension=0,
        tiled=True,
    ).astype(jnp.float32)
    norm_value, second_pull = jax.vjp(layer_norm, hidden_one, gain_second, bias_second)
    grad_hidden_norm, grad_gain_second, grad_bias_second = second_pull(grad_normed_two)
    grad_hidden = grad_out + grad_hidden_norm
    grad_out_bias = jnp.sum(grad_hidden, axis=0)
    grad_attn_low = grad_hidden.astype(jnp.bfloat16)
    grad_attn_rows = lax.all_gather(grad_attn_low, "tp", axis=0, tiled=True)
    grad_out_w = jnp.einsum(
        "nc,nd->cd", attended, grad_attn_rows, preferred_element_type=jnp.float32
    )
    grad_attended = jnp.einsum(
        "nd,cd->nc", grad_attn_rows, out_w, preferred_element_type=jnp.float32
    ).astype(jnp.bfloat16)
    grad_queries, grad_keys, grad_values = lax.map(
        backward_sequence,
        (
            shaped_queries,
            shaped_keys,
            shaped_values,
            segment_ids,
            log_totals,
            grad_attended.reshape(seq_count, block_count, block_rows, head_count, HD),
        ),
    )
    flat_queries = grad_queries.reshape(-1, head_count * HD)
    flat_keys = grad_keys.reshape(-1, head_count * HD)
    flat_values = grad_values.reshape(-1, head_count * HD)
    grad_query_w = jnp.einsum(
        "nd,nc->dc", rows_one, flat_queries, preferred_element_type=jnp.float32
    )
    grad_key_w = jnp.einsum("nd,nc->dc", rows_one, flat_keys, preferred_element_type=jnp.float32)
    grad_value_w = jnp.einsum(
        "nd,nc->dc", rows_one, flat_values, preferred_element_type=jnp.float32
    )
    grad_query_b = jnp.sum(flat_queries, axis=0, dtype=jnp.float32).reshape(query_b.shape)
    grad_value_b = jnp.sum(flat_values, axis=0, dtype=jnp.float32).reshape(value_b.shape)
    stacked_grads = jnp.concatenate((flat_queries, flat_keys, flat_values), axis=1)
    stacked_weights = jnp.concatenate((query_w, key_w, value_w), axis=1)
    grad_normed_one = lax.psum_scatter(
        jnp.einsum(
            "nc,dc->nd", stacked_grads, stacked_weights, preferred_element_type=jnp.float32
        ).astype(jnp.bfloat16),
        "tp",
        scatter_dimension=0,
        tiled=True,
    ).astype(jnp.float32)
    first_value, first_pull = jax.vjp(layer_norm, input_float, gain_first, bias_first)
    grad_input_norm, grad_gain_first, grad_bias_first = first_pull(grad_normed_one)
    grad_input = grad_hidden + grad_input_norm
    summed = lax.psum(
        (
            square_part,
            grad_gain_first,
            grad_bias_first,
            grad_out_bias,
            grad_gain_second,
            grad_bias_second,
            grad_lower_bias,
        ),
        ("fsdp", "tp"),
    )
    piece_size = D // fsdp_size
    piece_start = lax.axis_index("fsdp") * piece_size

    def own_piece(vector):
        return lax.dynamic_slice_in_dim(vector, piece_start, piece_size)

    loss = 0.5 * summed[0] / valid_total
    grad_wq, grad_wk, grad_wv, grad_bq, grad_bv, grad_wo, grad_wu, grad_bu, grad_wd = (
        lax.psum_scatter(
            grad_query_w.astype(jnp.bfloat16), "fsdp", scatter_dimension=0, tiled=True
        ).astype(jnp.float32),
        lax.psum_scatter(
            grad_key_w.astype(jnp.bfloat16), "fsdp", scatter_dimension=0, tiled=True
        ).astype(jnp.float32),
        lax.psum_scatter(
            grad_value_w.astype(jnp.bfloat16), "fsdp", scatter_dimension=0, tiled=True
        ).astype(jnp.float32),
        lax.psum_scatter(
            grad_query_b.astype(jnp.bfloat16), "fsdp", scatter_dimension=1, tiled=True
        ).astype(jnp.float32),
        lax.psum_scatter(
            grad_value_b.astype(jnp.bfloat16), "fsdp", scatter_dimension=1, tiled=True
        ).astype(jnp.float32),
        lax.psum_scatter(
            grad_out_w.astype(jnp.bfloat16), "fsdp", scatter_dimension=1, tiled=True
        ).astype(jnp.float32),
        lax.psum_scatter(
            grad_upper.astype(jnp.bfloat16), "fsdp", scatter_dimension=0, tiled=True
        ).astype(jnp.float32),
        lax.psum_scatter(
            grad_upper_bias.astype(jnp.bfloat16), "fsdp", scatter_dimension=1, tiled=True
        ).astype(jnp.float32),
        lax.psum_scatter(
            grad_lower.astype(jnp.bfloat16), "fsdp", scatter_dimension=1, tiled=True
        ).astype(jnp.float32),
    )
    return (
        out_full.astype(jnp.bfloat16),
        loss,
        grad_input,
        own_piece(summed[1]),
        own_piece(summed[2]),
        grad_wq,
        grad_wk,
        grad_wv,
        grad_bq,
        grad_bv,
        grad_wo,
        own_piece(summed[3]),
        own_piece(summed[4]),
        own_piece(summed[5]),
        grad_wu,
        grad_bu,
        grad_wd,
        own_piece(summed[6]),
    )


def solution(mesh):
    placed = (
        P(("fsdp", "tp"), None),
        P("fsdp", None),
        P(("fsdp", "tp")),
        P(("fsdp", "tp"), None),
        P(("fsdp", "tp"), None),
        P("fsdp"),
        P("fsdp"),
        P("fsdp", "tp"),
        P("fsdp", "tp"),
        P("fsdp", "tp"),
        P("tp", "fsdp"),
        P("tp", "fsdp"),
        P("tp", "fsdp"),
        P("fsdp"),
        P("fsdp"),
        P("fsdp"),
        P("fsdp", "tp"),
        P("tp", "fsdp"),
        P("tp", "fsdp"),
        P("fsdp"),
    )
    return jax.shard_map(
        local,
        mesh=mesh,
        in_specs=placed,
        out_specs=(
            P(("fsdp", "tp"), None),
            P(),
            P(("fsdp", "tp"), None),
            P("fsdp"),
            P("fsdp"),
            P("fsdp", "tp"),
            P("fsdp", "tp"),
            P("fsdp", "tp"),
            P("tp", "fsdp"),
            P("tp", "fsdp"),
            P("tp", "fsdp"),
            P("fsdp"),
            P("fsdp"),
            P("fsdp"),
            P("fsdp", "tp"),
            P("tp", "fsdp"),
            P("tp", "fsdp"),
            P("fsdp"),
        ),
        check_vma=False,
    )
```

profile of v0, /device:TPU:0, one launch (start us, length us, event | category | flops | bytes accessed | tf_op | source)
XLA Modules:
  0.0 948.7 jit_solution(11095047475518688719)
XLA Ops:
  14.4 16.0 %all-reduce.11 = (bf16[512]{0:T(512)(128)(2,1)}, bf16[512]{0:T(512)(128)(2,1)}, bf16[512]{0:T(512)(128)(2,1)}, bf16[512]{0:T(512)(128)(2,1)S(1)}, bf16[512]{0:T(512)(128)(2,1)S(1)}, /*index=5*/bf16[512]{0:T(512)(128)(2,1)}) all-reduce(bf16[512]{0:T(512)(128)(2,1)S(1)} %dynamic-update-slice.5, ...), channel_id=1, replica_groups=mesh['fsdp'=8,'tp'=4] {'fsdp'}, use_global_device_ids=true, to_apply=%add.5 | all-reduce | flops 3072 | bytes 12288
  88.5 10.3 %all-gather.7.cloned.1.call-done = bf16[3072,512]{1,0:T(8,128)(2,1)} async-done(((bf16[768,512]{1,0:T(8,128)(2,1)}), bf16[3072,512]{1,0:T(8,128)(2,1)}) %all-gather.7.cloned.1.call-update) | async-done | bytes 3145744 | tf_op jit(solution)/shard_map/all_gather | solution.py:158
  131.4 47.3 %while.54 = (s32[]{:T(128)}, bf16[3,2,512,2,64]{2,1,0,4,3:T(2,128)(2,1)}, f32[3,2,2,512]{3,2,1,0:T(2,128)}, bf16[3,2,512,2,64]{2,4,3,1,0:T(8,128)(2,1)S(1)}, s32...) while((s32[]{:T(128)}, ...), condition=%wide.region_7.8_spmd, body=%wide.region_2.7_spmd.sunk | while | flops 282656256 | bytes 17635796 | solution.py:174
  132.2 13.3 %while.57 = (s32[]{:T(128)}, bf16[2,512,2,64]{1,3,2,0:T(8,128)(2,1)S(1)}, f32[2,2,512]{2,1,0:T(2,128)S(1)}, s32[2]{0:T(128)S(1)}, s32[1024]{0:T(1024)S(1)}, /*in...) while((s32[]{:T(128)}, ...), condition=%wide.region_6.6_spmd, body=%wide.region_3.5_spmd.sunk | while | flops 282656256 | bytes 15513803 | solution.py:50
  148.0 13.3 %while.57 = (s32[]{:T(128)}, bf16[2,512,2,64]{1,3,2,0:T(8,128)(2,1)S(1)}, f32[2,2,512]{2,1,0:T(2,128)S(1)}, s32[2]{0:T(128)S(1)}, s32[1024]{0:T(1024)S(1)}, /*in...) while((s32[]{:T(128)}, ...), condition=%wide.region_6.6_spmd, body=%wide.region_3.5_spmd.sunk | while | flops 282656256 | bytes 15513803 | solution.py:50
  163.7 13.3 %while.57 = (s32[]{:T(128)}, bf16[2,512,2,64]{1,3,2,0:T(8,128)(2,1)S(1)}, f32[2,2,512]{2,1,0:T(2,128)S(1)}, s32[2]{0:T(128)S(1)}, s32[1024]{0:T(1024)S(1)}, /*in...) while((s32[]{:T(128)}, ...), condition=%wide.region_6.6_spmd, body=%wide.region_3.5_spmd.sunk | while | flops 282656256 | bytes 15513803 | solution.py:50
  184.9 58.4 %reduce-scatter.14.cloned.1.call-done = bf16[768,512]{1,0:T(8,128)(2,1)} async-done(((bf16[3072,512]{1,0:T(8,128)(2,1)}), bf16[768,512]{1,0:T(8,128)(2,1)}) %reduce-scatter.14.cloned.1.call-update) | async-done | bytes 786448 | tf_op jit(solution)/shard_map/reduce_scatter | solution.py:178
  255.8 10.8 %all_gather.70 = bf16[512,512]{1,0:T(8,128)(2,1)} all-gather(bf16[64,512]{1,0:T(8,128)(2,1)S(1)} %copy-done.38), channel_id=1, replica_groups=mesh['fsdp'=8,'tp'=4] {'fsdp'}, dimensions={0}, use_global_device_ids=true | all-gather | bytes 589824 | tf_op jit(solution)/shard_map/all_gather | solution.py:143
  276.6 33.8 %all-gather.9.cloned.1.call-done = bf16[3072,512]{1,0:T(8,128)(2,1)} async-done(((bf16[768,512]{1,0:T(8,128)(2,1)}), bf16[3072,512]{1,0:T(8,128)(2,1)}) %all-gather.9.cloned.1.call-update) | async-done | bytes 3145744 | tf_op jit(solution)/shard_map/all_gather | solution.py:186
  324.3 42.1 %psum.57 = f32[]{:T(128)} all-reduce(f32[]{:T(128)} %convert_reduce_fusion.3), channel_id=1, replica_groups=mesh['fsdp'=8,'tp'=4] {'fsdp','tp'}, use_global_device_ids=true, to_apply=%region_16.17 | all-reduce | flops 1 | bytes 8 | tf_op jit(solution)/shard_map/psum | solution.py:149
  367.1 15.9 %reduce-scatter.16.cloned.1.call-done = bf16[768,512]{1,0:T(8,128)(2,1)} async-done(((bf16[3072,512]{1,0:T(8,128)(2,1)}), bf16[768,512]{1,0:T(8,128)(2,1)}) %reduce-scatter.16.cloned.1.call-update) | async-done | bytes 786448 | tf_op jit(solution)/shard_map/reduce_scatter | solution.py:191
  388.3 63.5 %all-gather.11.cloned.1.call-done = bf16[3072,512]{1,0:T(8,128)(2,1)} async-done(((bf16[768,512]{1,0:T(8,128)(2,1)}), bf16[3072,512]{1,0:T(8,128)(2,1)}) %all-gather.11.cloned.1.call-update) | async-done | bytes 3145744 | tf_op jit(solution)/shard_map/all_gather | solution.py:205
  465.9 59.0 %reduce-scatter.18.cloned.1.call-done = bf16[768,512]{1,0:T(8,128)(2,1)} async-done(((bf16[3072,512]{1,0:T(8,128)(2,1)}), bf16[768,512]{1,0:T(8,128)(2,1)}) %reduce-scatter.18.cloned.1.call-update) | async-done | bytes 786448 | tf_op jit(solution)/shard_map/reduce_scatter | solution.py:214
  546.0 52.0 %all-gather.13.cloned.1.call-done = bf16[3072,512]{1,0:T(8,128)(2,1)} async-done(((bf16[768,512]{1,0:T(8,128)(2,1)}), bf16[3072,512]{1,0:T(8,128)(2,1)}) %all-gather.13.cloned.1.call-update) | async-done | bytes 3145744 | tf_op jit(solution)/shard_map/all_gather | solution.py:227
  607.9 69.2 %while.56 = (s32[]{:T(128)}, bf16[3,2,512,2,64]{2,4,3,1,0:T(8,128)(2,1)}, bf16[3,1024,2,64]{1,3,2,0:T(8,128)(2,1)}, bf16[3,1024,2,64]{1,3,2,0:T(8,128)(2,1)}, bf...) while((s32[]{:T(128)}, ...), condition=%wide.region_24.25_spmd, body=%wide.region_20.24_spmd.sunk | while | flops 689438208 | bytes 45550196 | solution.py:234
  610.6 17.6 %while.58 = (s32[]{:T(128)}, f32[1024,2,64]{0,2,1:T(8,128)S(1)}, f32[1024,2,64]{0,2,1:T(8,128)}, bf16[2,512,2,64]{1,3,2,0:T(8,128)(2,1)S(1)}, bf16[2,512,2,64]{1...) while((s32[]{:T(128)}, f32[1024,2,64]{0,2,1:T(8,128)S(1)}, ...), condition=%wide.region_23.23_spmd.clone, body=%wide.region_21.22_spmd.clone.sunk | while | flops 689176064 | bytes 41330992 | solution.py:82
  633.7 17.6 %while.58 = (s32[]{:T(128)}, f32[1024,2,64]{0,2,1:T(8,128)S(1)}, f32[1024,2,64]{0,2,1:T(8,128)}, bf16[2,512,2,64]{1,3,2,0:T(8,128)(2,1)S(1)}, bf16[2,512,2,64]{1...) while((s32[]{:T(128)}, f32[1024,2,64]{0,2,1:T(8,128)S(1)}, ...), condition=%wide.region_23.23_spmd.clone, body=%wide.region_21.22_spmd.clone.sunk | while | flops 689176064 | bytes 41330992 | solution.py:82
  656.8 17.6 %while.58 = (s32[]{:T(128)}, f32[1024,2,64]{0,2,1:T(8,128)S(1)}, f32[1024,2,64]{0,2,1:T(8,128)}, bf16[2,512,2,64]{1,3,2,0:T(8,128)(2,1)S(1)}, bf16[2,512,2,64]{1...) while((s32[]{:T(128)}, f32[1024,2,64]{0,2,1:T(8,128)S(1)}, ...), condition=%wide.region_23.23_spmd.clone, body=%wide.region_21.22_spmd.clone.sunk | while | flops 689176064 | bytes 41330992 | solution.py:82
  705.8 13.7 %all-reduce.10 = (bf16[2,64]{1,0:T(2,128)(2,1)S(1)}, bf16[2,64]{1,0:T(2,128)(2,1)S(1)}, bf16[8,64]{1,0:T(8,128)(2,1)S(1)}) all-reduce(bf16[2,64]{1,0:T(2,128)(2,1)S(1)} %reduce_sum.233, bf16[2,64]{1,0:T(2,128)(2,1)S(1)} %reduce_sum.234, bf16[8,64]{1,0:T(8,128)(2,1)S(1)} %convert_element_type.247), channel_id=9, replica_groups=mesh['fsdp'=8,'tp'=4] {'fsdp'}, use_global_device_ids=true, to_apply=%region_36.37.clone | all-reduce | flops 768 | bytes 3072
  722.1 33.2 %reduce-scatter.22.cloned.1.call-done = bf16[64,128]{1,0:T(8,128)(2,1)} async-done(((bf16[512,128]{1,0:T(8,128)(2,1)}), bf16[64,128]{1,0:T(8,128)(2,1)}) %reduce-scatter.22.cloned.1.call-update) | async-done | bytes 16400 | tf_op jit(solution)/shard_map/reduce_scatter | solution.py:290
  756.6 34.9 %reduce-scatter.26.cloned.1.call-done = bf16[64,128]{1,0:T(8,128)(2,1)} async-done(((bf16[512,128]{1,0:T(8,128)(2,1)}), bf16[64,128]{1,0:T(8,128)(2,1)}) %reduce-scatter.26.cloned.1.call-update) | async-done | bytes 16400 | tf_op jit(solution)/shard_map/reduce_scatter | solution.py:296
  792.9 35.3 %reduce-scatter.24.cloned.1.call-done = bf16[64,128]{1,0:T(8,128)(2,1)} async-done(((bf16[512,128]{1,0:T(8,128)(2,1)}), bf16[64,128]{1,0:T(8,128)(2,1)}) %reduce-scatter.24.cloned.1.call-update) | async-done | bytes 16400 | tf_op jit(solution)/shard_map/reduce_scatter | solution.py:293
  829.6 61.1 %reduce-scatter.20.cloned.1.call-done = bf16[768,512]{1,0:T(8,128)(2,1)} async-done(((bf16[3072,512]{1,0:T(8,128)(2,1)}), bf16[768,512]{1,0:T(8,128)(2,1)}) %reduce-scatter.20.cloned.1.call-update) | async-done | bytes 786448 | tf_op jit(solution)/shard_map/reduce_scatter | solution.py:259
  893.4 40.6 %all-reduce.9 = (f32[]{:T(128)}, f32[512]{0:T(512)S(1)}, f32[512]{0:T(512)S(1)}, f32[512]{0:T(512)S(1)}, f32[512]{0:T(512)S(1)}, /*index=5*/f32[512]{0:T(512)S(1)}, f32[512]{0:T(512)S(1)}) all-reduce(f32[]{:T(128)} %multiply_reduce_fusion.3, f32[512]{0:T(512)S(1)} %get-tuple-element.340, ...), channel_id=1, replica_groups=mesh['fsdp'=8,'tp'=4] {'fsdp','tp'}, use_global_device_ids=true, to_apply=%region_14.15 | all-reduce | flops 3073 | bytes 24584 | tf_op jit(solution)/shard_map/psum | solution.py:270
  (474 shorter events, 339.5 us)
Async XLA Ops:
  7.2 91.5 %all-gather.7.cloned.1.call-start = ((), (), s32[]{:S(2)}) async-start(), calls=%async_computation.10 | async-start | bytes 3932160 | tf_op jit(solution)/shard_map/all_gather | solution.py:158
  35.7 207.5 %reduce-scatter.14.cloned.1.call-start = ((), (), s32[]{:S(2)}) async-start(), calls=%async_computation.11 | async-start | bytes 3932160 | tf_op jit(solution)/shard_map/reduce_scatter | solution.py:178
  184.2 126.2 %all-gather.9.cloned.1.call-start = ((), (), s32[]{:S(2)}) async-start(), calls=%async_computation.12 | async-start | bytes 3932160 | tf_op jit(solution)/shard_map/all_gather | solution.py:186
  246.7 136.3 %reduce-scatter.16.cloned.1.call-start = ((), (), s32[]{:S(2)}) async-start(), calls=%async_computation.13 | async-start | bytes 3932160 | tf_op jit(solution)/shard_map/reduce_scatter | solution.py:191
  323.0 128.8 %all-gather.11.cloned.1.call-start = ((), (), s32[]{:S(2)}) async-start(), calls=%async_computation.14 | async-start | bytes 3932160 | tf_op jit(solution)/shard_map/all_gather | solution.py:205
  388.1 136.9 %reduce-scatter.18.cloned.1.call-start = ((), (), s32[]{:S(2)}) async-start(), calls=%async_computation.15 | async-start | bytes 3932160 | tf_op jit(solution)/shard_map/reduce_scatter | solution.py:214
  465.9 132.1 %all-gather.13.cloned.1.call-start = ((), (), s32[]{:S(2)}) async-start(), calls=%async_computation.16 | async-start | bytes 3932160 | tf_op jit(solution)/shard_map/all_gather | solution.py:227
  534.3 167.4 %reduce-scatter.32.cloned.1.call-start = ((), (), s32[]{:S(2)}) async-start(), calls=%async_computation.23 | async-start | bytes 589824 | tf_op jit(solution)/shard_map/reduce_scatter | solution.py:314
  539.9 163.3 %reduce-scatter.30.cloned.1.call-start = ((), (), s32[]{:S(2)}) async-start(), calls=%async_computation.22 | async-start | bytes 589824 | tf_op jit(solution)/shard_map/reduce_scatter | solution.py:308
  546.0 174.8 %reduce-scatter.28.cloned.1.call-start = ((), (), s32[]{:S(2)}) async-start(), calls=%async_computation.21 | async-start | bytes 147456 | tf_op jit(solution)/shard_map/reduce_scatter | solution.py:305
  686.5 68.8 %reduce-scatter.22.cloned.1.call-start = ((), (), s32[]{:S(2)}) async-start(), calls=%async_computation.18 | async-start | bytes 147456 | tf_op jit(solution)/shard_map/reduce_scatter | solution.py:290
  689.6 101.9 %reduce-scatter.26.cloned.1.call-start = ((), (), s32[]{:S(2)}) async-start(), calls=%async_computation.20 | async-start | bytes 147456 | tf_op jit(solution)/shard_map/reduce_scatter | solution.py:296
  692.5 135.7 %reduce-scatter.24.cloned.1.call-start = ((), (), s32[]{:S(2)}) async-start(), calls=%async_computation.19 | async-start | bytes 147456 | tf_op jit(solution)/shard_map/reduce_scatter | solution.py:293
  695.5 195.2 %reduce-scatter.20.cloned.1.call-start = ((), (), s32[]{:S(2)}) async-start(), calls=%async_computation.17 | async-start | bytes 3932160 | tf_op jit(solution)/shard_map/reduce_scatter | solution.py:259
  700.7 190.0 %copy-start.2 = (bf16[768,512]{1,0:T(8,128)(2,1)S(1)}, bf16[768,512]{1,0:T(8,128)(2,1)}, u32[]{:S(2)}) copy-start(bf16[768,512]{1,0:T(8,128)(2,1)} %param.28) | copy-start | bytes 2359300
  700.7 189.9 %copy-start.36 = (f32[768]{0:T(1024)S(1)}, f32[768]{0:T(1024)}, u32[]{:S(2)}) copy-start(f32[768]{0:T(1024)} %copy-done.35) | copy-start | bytes 9220
  700.7 189.9 %copy-start.43 = (f32[512]{0:T(512)S(1)}, f32[512]{0:T(512)}, u32[]{:S(2)}) copy-start(f32[512]{0:T(512)} %copy-done.42) | copy-start | bytes 6148
  700.8 191.7 %copy-start.45 = (f32[768]{0:T(1024)S(1)}, f32[768]{0:T(1024)}, u32[]{:S(2)}) copy-start(f32[768]{0:T(1024)} %copy-done.44) | copy-start | bytes 9220
  700.8 191.7 %copy-start.41 = (f32[768]{0:T(1024)S(1)}, f32[768]{0:T(1024)}, u32[]{:S(2)}) copy-start(f32[768]{0:T(1024)} %copy-done.40) | copy-start | bytes 9220
  705.5 187.9 %copy-start.53 = (f32[512]{0:T(512)S(1)}, f32[512]{0:T(512)}, u32[]{:S(2)}) copy-start(f32[512]{0:T(512)} %get-tuple-element.437) | copy-start | bytes 6148
  705.5 187.9 %copy-start.54 = (f32[512]{0:T(512)S(1)}, f32[512]{0:T(512)}, u32[]{:S(2)}) copy-start(f32[512]{0:T(512)} %get-tuple-element.338) | copy-start | bytes 6148
  705.5 187.9 %copy-start.55 = (f32[512]{0:T(512)S(1)}, f32[512]{0:T(512)}, u32[]{:S(2)}) copy-start(f32[512]{0:T(512)} %get-tuple-element.439) | copy-start | bytes 6148
  705.5 187.9 %copy-start.56 = (f32[512]{0:T(512)S(1)}, f32[512]{0:T(512)}, u32[]{:S(2)}) copy-start(f32[512]{0:T(512)} %get-tuple-element.343) | copy-start | bytes 6148
  705.5 233.4 %copy-start.11 = (f32[768,512]{1,0:T(8,128)S(1)}, f32[768,512]{1,0:T(8,128)}, u32[]{:S(2)}) copy-start(f32[768,512]{1,0:T(8,128)} %copy-done.10) | copy-start | bytes 4718596
  (67 other events, 708.7 us)
Sparse Core Ops, SparseCore 0:
  35.8 62.8 all-gather.6
  184.3 58.8 reduce-scatter.13
  246.8 63.5 all-gather.8
  323.2 59.8 reduce-scatter.15
  388.2 63.5 all-gather.10
  466.0 58.8 reduce-scatter.17
  534.4 63.5 all-gather.12
  601.1 32.8 reduce-scatter.31
  637.4 34.1 reduce-scatter.29
  686.6 31.9 reduce-scatter.27
  721.9 33.3 reduce-scatter.21
  758.2 33.3 reduce-scatter.25
  794.8 33.3 reduce-scatter.23
  830.4 60.2 reduce-scatter.19
where the time goes:
time: 957 us; the launch traced here: 949 us
  waiting for transfers between devices  458 us (48%)
  blocking collectives  194 us (20%)
  matrix products  117 us (12%)
  local copies, waits for them, and re-layouts  86.9 us (9%)
  other arithmetic  63 us (7%)
  between operations  19.7 us (2%)
    all_gather x1, waiting for transfers between devices, local(): grad_rows = lax.all_gather(grad_out_low, 'tp', axis=0, tiled=True)  63.5 us
    reduce_scatter x1, waiting for transfers between devices, local(): lax.psum_scatter(jnp.einsum('nc,dc->nd', stacked_grads, stacked_weights,...  61.1 us
    reduce_scatter x1, waiting for transfers between devices, local(): lax.psum_scatter(jnp.einsum('nf,df->nd', grad_pre, upper_w, preferred_ele...  59 us
    reduce_scatter x1, waiting for transfers between devices, local(): lax.psum_scatter(jnp.dot(attended, out_w, preferred_element_type=jnp.floa...  58.4 us
    all_gather x1, waiting for transfers between devices, local(): grad_attn_rows = lax.all_gather(grad_attn_low, 'tp', axis=0, tiled=True)  52 us
    psum x1, blocking collectives, local(): valid_total = lax.psum(jnp.sum(mask_float), ('fsdp', 'tp'))  42.1 us
    psum x1, blocking collectives, local(): lax.psum((square_part, grad_gain_first, grad_bias_first, grad_out_bias, g...  40.6 us
    reduce_scatter x1, waiting for transfers between devices, local(): lax.psum_scatter(grad_key_w.astype(jnp.bfloat16), 'fsdp', scatter_dimensi...  35.3 us
  transfers between devices with their start and end apart: 14, of which 11 were waited for; matrix products, arithmetic and copies ran while one was open for 13% of the time, Pallas kernels for 0%

commit v1 on v0

--- a/solution.py
+++ b/solution.py
@@ -183,7 +183,14 @@
     ).astype(jnp.float32)
     hidden_one = input_float + attention + out_b.astype(jnp.float32)
     normed_two = layer_norm(hidden_one, gain_second, bias_second).astype(jnp.bfloat16)
-    rows_two = lax.all_gather(normed_two, "tp", axis=0, tiled=True)
+    ways, here, step = (lax.axis_size("tp"), lax.axis_index("tp"), normed_two.shape[0])
+    line, have = (normed_two, 1)
+    while have < ways:
+        line = jnp.concatenate(
+            [line, lax.ppermute(line, "tp", [(d, (d - have) % ways) for d in range(ways)])], axis=0
+        )
+        have = 2 * have
+    rows_two = jnp.roll(line, here * step, axis=0)
     pre_act = jnp.dot(rows_two, upper_w, preferred_element_type=jnp.float32) + upper_b.reshape(
         -1
     ).astype(jnp.float32)

time: 957 us -> 1000 us (1.045)
  waiting for transfers between devices: 458 us -> 480 us
  matrix products: 117 us -> 130 us
    ppermute x0 -> x2, waiting for transfers between devices: none -> 56 us  [local(): lax.ppermute(line, 'tp', [(d, (d - have) % ways) for d in range(ways)])]
    all_gather x1 -> x0, waiting for transfers between devices: 33.8 us -> none  [local(): rows_two = lax.all_gather(normed_two, 'tp', axis=0, tiled=True)]
    dot_general x6, matrix products: 8.33 us -> 19.4 us  [backward_one_block(): jnp.einsum('hqk,qhd->khd', weights.astype(jnp.bfloat16), grad_block, pref...]
    unnamed x146 -> x148, local copies, waits for them, and re-layouts: 16.9 us -> 23.4 us
  transfers between devices with their start and end apart: 14 -> 15, of which waited for: 11 -> 12; matrix products, arithmetic and copies ran while one was open for 13% -> 14% of each run, Pallas kernels for 0% -> 0%
where the time goes in v1:
time: 1000 us; the launch traced here: 996 us
  waiting for transfers between devices  480 us (48%)
  blocking collectives  195 us (20%)
  matrix products  130 us (13%)
  local copies, waits for them, and re-layouts  91.7 us (9%)
  other arithmetic  64.2 us (6%)
  between operations  19.6 us (2%)
    all_gather x1, waiting for transfers between devices, local(): grad_rows = lax.all_gather(grad_out_low, 'tp', axis=0, tiled=True)  63.5 us
    reduce_scatter x1, waiting for transfers between devices, local(): lax.psum_scatter(jnp.einsum('nc,dc->nd', stacked_grads, stacked_weights,...  61.3 us
    reduce_scatter x1, waiting for transfers between devices, local(): lax.psum_scatter(jnp.einsum('nf,df->nd', grad_pre, upper_w, preferred_ele...  59 us
    reduce_scatter x1, waiting for transfers between devices, local(): lax.psum_scatter(jnp.dot(attended, out_w, preferred_element_type=jnp.floa...  58.4 us
    ppermute x2, waiting for transfers between devices, local(): lax.ppermute(line, 'tp', [(d, (d - have) % ways) for d in range(ways)])  56 us
    all_gather x1, waiting for transfers between devices, local(): grad_attn_rows = lax.all_gather(grad_attn_low, 'tp', axis=0, tiled=True)  51.8 us
    psum x1, blocking collectives, local(): valid_total = lax.psum(jnp.sum(mask_float), ('fsdp', 'tp'))  44.4 us
    psum x1, blocking collectives, local(): lax.psum((square_part, grad_gain_first, grad_bias_first, grad_out_bias, g...  40.7 us
  transfers between devices with their start and end apart: 15, of which 12 were waited for; matrix products, arithmetic and copies ran while one was open for 14% of the time, Pallas kernels for 0%

profile of v1, /device:TPU:0, one launch (start us, length us, event | category | flops | bytes accessed | tf_op | source)
XLA Modules:
  0.0 995.7 jit_solution(14871553443377704452)
XLA Ops:
  14.4 16.0 %all-reduce.11 = (bf16[512]{0:T(512)(128)(2,1)}, bf16[512]{0:T(512)(128)(2,1)}, bf16[512]{0:T(512)(128)(2,1)}, bf16[512]{0:T(512)(128)(2,1)S(1)}, bf16[512]{0:T(512)(128)(2,1)S(1)}, /*index=5*/bf16[512]{0:T(512)(128)(2,1)}) all-reduce(bf16[512]{0:T(512)(128)(2,1)S(1)} %dynamic-update-slice.5, ...), channel_id=1, replica_groups=mesh['fsdp'=8,'tp'=4] {'fsdp'}, use_global_device_ids=true, to_apply=%add.5 | all-reduce | flops 3072 | bytes 12288
  88.4 10.3 %all-gather.6.cloned.1.call-done = bf16[3072,512]{1,0:T(8,128)(2,1)} async-done(((bf16[768,512]{1,0:T(8,128)(2,1)}), bf16[3072,512]{1,0:T(8,128)(2,1)}) %all-gather.6.cloned.1.call-update) | async-done | bytes 3145744 | tf_op jit(solution)/shard_map/all_gather | solution.py:158
  128.2 41.5 %while.54 = (s32[]{:T(128)}, bf16[3,2,512,2,64]{2,1,0,4,3:T(2,128)(2,1)S(1)}, f32[3,2,2,512]{3,2,1,0:T(2,128)S(1)}, bf16[3,2,512,2,64]{2,4,3,1,0:T(8,128)(2,1)},...) while((s32[]{:T(128)}, ...), condition=%wide.region_7.8_spmd, body=%wide.region_2.7_spmd.sunk | while | flops 282656256 | bytes 17635780 | solution.py:174
  130.3 11.4 %while.57 = (s32[]{:T(128)}, bf16[2,512,2,64]{1,3,2,0:T(8,128)(2,1)S(1)}, f32[2,2,512]{2,1,0:T(2,128)S(1)}, s32[2]{0:T(128)S(1)}, s32[1024]{0:T(1024)S(1)}, /*in...) while((s32[]{:T(128)}, ...), condition=%wide.region_6.6_spmd, body=%wide.region_3.5_spmd.sunk | while | flops 282656256 | bytes 15513795 | solution.py:50
  144.1 11.4 %while.57 = (s32[]{:T(128)}, bf16[2,512,2,64]{1,3,2,0:T(8,128)(2,1)S(1)}, f32[2,2,512]{2,1,0:T(2,128)S(1)}, s32[2]{0:T(128)S(1)}, s32[1024]{0:T(1024)S(1)}, /*in...) while((s32[]{:T(128)}, ...), condition=%wide.region_6.6_spmd, body=%wide.region_3.5_spmd.sunk | while | flops 282656256 | bytes 15513795 | solution.py:50
  157.9 11.4 %while.57 = (s32[]{:T(128)}, bf16[2,512,2,64]{1,3,2,0:T(8,128)(2,1)S(1)}, f32[2,2,512]{2,1,0:T(2,128)S(1)}, s32[2]{0:T(128)S(1)}, s32[1024]{0:T(1024)S(1)}, /*in...) while((s32[]{:T(128)}, ...), condition=%wide.region_6.6_spmd, body=%wide.region_3.5_spmd.sunk | while | flops 282656256 | bytes 15513795 | solution.py:50
  174.6 58.4 %reduce-scatter.14.cloned.1.call-done = bf16[768,512]{1,0:T(8,128)(2,1)} async-done(((bf16[3072,512]{1,0:T(8,128)(2,1)}), bf16[768,512]{1,0:T(8,128)(2,1)}) %reduce-scatter.14.cloned.1.call-update) | async-done | bytes 786448 | tf_op jit(solution)/shard_map/reduce_scatter | solution.py:178
  238.6 17.0 %collective-permute-done = bf16[768,512]{1,0:T(8,128)(2,1)S(1)} collective-permute-done((bf16[768,512]{1,0:T(8,128)(2,1)S(1)}, bf16[768,512]{1,0:T(8,128)(2,1)S(1)}, u32[]{:S(2)}, u32[]{:S(2)}) %collective-permute-start) | collective-permute-done | bytes 786464 | tf_op jit(solution)/shard_map/ppermute | solution.py:190
  288.3 39.0 %collective-permute-done.1 = bf16[1536,512]{1,0:T(8,128)(2,1)} collective-permute-done((bf16[1536,512]{1,0:T(8,128)(2,1)}, bf16[1536,512]{1,0:T(8,128)(2,1)}, u32[]{:S(2)}, u32[]{:S(2)}) %collective-permute-start.1) | collective-permute-done | bytes 1572896 | tf_op jit(solution)/shard_map/ppermute | solution.py:190
  348.2 44.4 %psum.57 = f32[]{:T(128)} all-reduce(f32[]{:T(128)} %convert_reduce_fusion.3), channel_id=1, replica_groups=mesh['fsdp'=8,'tp'=4] {'fsdp','tp'}, use_global_device_ids=true, to_apply=%region_16.17 | all-reduce | flops 1 | bytes 8 | tf_op jit(solution)/shard_map/psum | solution.py:149
  393.3 15.9 %reduce-scatter.16.cloned.1.call-done = bf16[768,512]{1,0:T(8,128)(2,1)} async-done(((bf16[3072,512]{1,0:T(8,128)(2,1)}), bf16[768,512]{1,0:T(8,128)(2,1)}) %reduce-scatter.16.cloned.1.call-update) | async-done | bytes 786448 | tf_op jit(solution)/shard_map/reduce_scatter | solution.py:198
  414.3 63.5 %all-gather.8.cloned.1.call-done = bf16[3072,512]{1,0:T(8,128)(2,1)} async-done(((bf16[768,512]{1,0:T(8,128)(2,1)}), bf16[3072,512]{1,0:T(8,128)(2,1)}) %all-gather.8.cloned.1.call-update) | async-done | bytes 3145744 | tf_op jit(solution)/shard_map/all_gather | solution.py:212
  491.8 59.0 %reduce-scatter.18.cloned.1.call-done = bf16[768,512]{1,0:T(8,128)(2,1)} async-done(((bf16[3072,512]{1,0:T(8,128)(2,1)}), bf16[768,512]{1,0:T(8,128)(2,1)}) %reduce-scatter.18.cloned.1.call-update) | async-done | bytes 786448 | tf_op jit(solution)/shard_map/reduce_scatter | solution.py:221
  572.1 51.8 %all-gather.10.cloned.1.call-done = bf16[3072,512]{1,0:T(8,128)(2,1)} async-done(((bf16[768,512]{1,0:T(8,128)(2,1)}), bf16[3072,512]{1,0:T(8,128)(2,1)}) %all-gather.10.cloned.1.call-update) | async-done | bytes 3145744 | tf_op jit(solution)/shard_map/all_gather | solution.py:234
  628.6 93.1 %while.56 = (s32[]{:T(128)}, bf16[3,2,512,2,64]{2,4,3,1,0:T(8,128)(2,1)}, bf16[3,1024,2,64]{1,3,2,0:T(8,128)(2,1)}, bf16[3,1024,2,64]{1,3,2,0:T(8,128)(2,1)}, bf...) while((s32[]{:T(128)}, ...), condition=%wide.region_24.25_spmd, body=%wide.region_20.24_spmd.sunk | while | flops 689438208 | bytes 95884224 | solution.py:241
  631.0 24.9 %while.58 = (s32[]{:T(128)}, f32[1024,2,64]{0,2,1:T(8,128)S(1)}, f32[1024,2,64]{0,2,1:T(8,128)}, bf16[2,512,2,64]{1,3,2,0:T(8,128)(2,1)}, bf16[2,512,2,64]{1,3,2...) while((s32[]{:T(128)}, f32[1024,2,64]{0,2,1:T(8,128)S(1)}, ...), condition=%wide.region_23.23_spmd.clone, body=%wide.region_21.22_spmd.clone.sunk | while | flops 689176064 | bytes 79080984 | solution.py:82
  662.0 24.9 %while.58 = (s32[]{:T(128)}, f32[1024,2,64]{0,2,1:T(8,128)S(1)}, f32[1024,2,64]{0,2,1:T(8,128)}, bf16[2,512,2,64]{1,3,2,0:T(8,128)(2,1)}, bf16[2,512,2,64]{1,3,2...) while((s32[]{:T(128)}, f32[1024,2,64]{0,2,1:T(8,128)S(1)}, ...), condition=%wide.region_23.23_spmd.clone, body=%wide.region_21.22_spmd.clone.sunk | while | flops 689176064 | bytes 79080984 | solution.py:82
  693.0 24.9 %while.58 = (s32[]{:T(128)}, f32[1024,2,64]{0,2,1:T(8,128)S(1)}, f32[1024,2,64]{0,2,1:T(8,128)}, bf16[2,512,2,64]{1,3,2,0:T(8,128)(2,1)}, bf16[2,512,2,64]{1,3,2...) while((s32[]{:T(128)}, f32[1024,2,64]{0,2,1:T(8,128)S(1)}, ...), condition=%wide.region_23.23_spmd.clone, body=%wide.region_21.22_spmd.clone.sunk | while | flops 689176064 | bytes 79080984 | solution.py:82
  752.7 13.8 %all-reduce.10 = (bf16[2,64]{1,0:T(2,128)(2,1)S(1)}, bf16[2,64]{1,0:T(2,128)(2,1)S(1)}, bf16[8,64]{1,0:T(8,128)(2,1)S(1)}) all-reduce(bf16[2,64]{1,0:T(2,128)(2,1)S(1)} %reduce_sum.233, bf16[2,64]{1,0:T(2,128)(2,1)S(1)} %reduce_sum.234, bf16[8,64]{1,0:T(8,128)(2,1)S(1)} %convert_element_type.247), channel_id=9, replica_groups=mesh['fsdp'=8,'tp'=4] {'fsdp'}, use_global_device_ids=true, to_apply=%region_36.37.clone | all-reduce | flops 768 | bytes 3072
  769.1 32.9 %reduce-scatter.24.cloned.1.call-done = bf16[64,128]{1,0:T(8,128)(2,1)} async-done(((bf16[512,128]{1,0:T(8,128)(2,1)}), bf16[64,128]{1,0:T(8,128)(2,1)}) %reduce-scatter.24.cloned.1.call-update) | async-done | bytes 16400 | tf_op jit(solution)/shard_map/reduce_scatter | solution.py:300
  803.4 35.1 %reduce-scatter.26.cloned.1.call-done = bf16[64,128]{1,0:T(8,128)(2,1)} async-done(((bf16[512,128]{1,0:T(8,128)(2,1)}), bf16[64,128]{1,0:T(8,128)(2,1)}) %reduce-scatter.26.cloned.1.call-update) | async-done | bytes 16400 | tf_op jit(solution)/shard_map/reduce_scatter | solution.py:303
  839.8 35.2 %reduce-scatter.22.cloned.1.call-done = bf16[64,128]{1,0:T(8,128)(2,1)} async-done(((bf16[512,128]{1,0:T(8,128)(2,1)}), bf16[64,128]{1,0:T(8,128)(2,1)}) %reduce-scatter.22.cloned.1.call-update) | async-done | bytes 16400 | tf_op jit(solution)/shard_map/reduce_scatter | solution.py:297
  876.3 61.3 %reduce-scatter.20.cloned.1.call-done = bf16[768,512]{1,0:T(8,128)(2,1)} async-done(((bf16[3072,512]{1,0:T(8,128)(2,1)}), bf16[768,512]{1,0:T(8,128)(2,1)}) %reduce-scatter.20.cloned.1.call-update) | async-done | bytes 786448 | tf_op jit(solution)/shard_map/reduce_scatter | solution.py:266
  940.4 40.7 %all-reduce.9 = (f32[]{:T(128)}, f32[512]{0:T(512)S(1)}, f32[512]{0:T(512)S(1)}, f32[512]{0:T(512)S(1)}, f32[512]{0:T(512)S(1)}, /*index=5*/f32[512]{0:T(512)S(1)}, f32[512]{0:T(512)S(1)}) all-reduce(f32[]{:T(128)} %multiply_reduce_fusion.3, f32[512]{0:T(512)S(1)} %get-tuple-element.340, ...), channel_id=1, replica_groups=mesh['fsdp'=8,'tp'=4] {'fsdp','tp'}, use_global_device_ids=true, to_apply=%region_14.15 | all-reduce | flops 3073 | bytes 24584 | tf_op jit(solution)/shard_map/psum | solution.py:277
  (599 shorter events, 372.2 us)
Async XLA Ops:
  7.2 91.5 %all-gather.6.cloned.1.call-start = ((), (), s32[]{:S(2)}) async-start(), calls=%async_computation.10 | async-start | bytes 3932160 | tf_op jit(solution)/shard_map/all_gather | solution.py:158
  35.7 197.3 %reduce-scatter.14.cloned.1.call-start = ((), (), s32[]{:S(2)}) async-start(), calls=%async_computation.11 | async-start | bytes 3932160 | tf_op jit(solution)/shard_map/reduce_scatter | solution.py:178
  174.0 235.3 %reduce-scatter.16.cloned.1.call-start = ((), (), s32[]{:S(2)}) async-start(), calls=%async_computation.12 | async-start | bytes 3932160 | tf_op jit(solution)/shard_map/reduce_scatter | solution.py:198
  236.4 19.2 %collective-permute-start = (bf16[768,512]{1,0:T(8,128)(2,1)S(1)}, bf16[768,512]{1,0:T(8,128)(2,1)S(1)}, u32[]{:S(2)}, u32[]{:S(2)}) collective-permute-start(bf16[768,512]{1,0:T(8,128)(2,1)S(1)} %get-tuple-element.442), channel_id=1, source_target_pairs={{0,3},{1,0},{2,1},{3,2},{4,7},{5,4},{6,5},{7,6},{8,11},{9,8},{10,9... | collective-permute-start | bytes 2359304 | tf_op jit(solution)/shard_map/ppermute | solution.py:190
  256.9 70.4 %collective-permute-start.1 = (bf16[1536,512]{1,0:T(8,128)(2,1)}, bf16[1536,512]{1,0:T(8,128)(2,1)}, u32[]{:S(2)}, u32[]{:S(2)}) collective-permute-start(bf16[1536,512]{1,0:T(8,128)(2,1)} %pad_maximum_fusion), channel_id=1, source_target_pairs={{0,2},{1,3},{2,0},{3,1},{4,6},{5,7},{6,4},{7,5},{8,10},{9,11},{10,... | collective-permute-start | bytes 4718600 | tf_op jit(solution)/shard_map/ppermute | solution.py:190
  347.0 130.8 %all-gather.8.cloned.1.call-start = ((), (), s32[]{:S(2)}) async-start(), calls=%async_computation.13 | async-start | bytes 3932160 | tf_op jit(solution)/shard_map/all_gather | solution.py:212
  414.0 136.8 %reduce-scatter.18.cloned.1.call-start = ((), (), s32[]{:S(2)}) async-start(), calls=%async_computation.14 | async-start | bytes 3932160 | tf_op jit(solution)/shard_map/reduce_scatter | solution.py:221
  491.8 132.1 %all-gather.10.cloned.1.call-start = ((), (), s32[]{:S(2)}) async-start(), calls=%async_computation.15 | async-start | bytes 3932160 | tf_op jit(solution)/shard_map/all_gather | solution.py:234
  560.2 188.4 %reduce-scatter.32.cloned.1.call-start = ((), (), s32[]{:S(2)}) async-start(), calls=%async_computation.22 | async-start | bytes 589824 | tf_op jit(solution)/shard_map/reduce_scatter | solution.py:321
  565.8 184.4 %reduce-scatter.30.cloned.1.call-start = ((), (), s32[]{:S(2)}) async-start(), calls=%async_computation.21 | async-start | bytes 589824 | tf_op jit(solution)/shard_map/reduce_scatter | solution.py:315
  571.8 195.9 %reduce-scatter.28.cloned.1.call-start = ((), (), s32[]{:S(2)}) async-start(), calls=%async_computation.20 | async-start | bytes 147456 | tf_op jit(solution)/shard_map/reduce_scatter | solution.py:312
  733.3 68.7 %reduce-scatter.24.cloned.1.call-start = ((), (), s32[]{:S(2)}) async-start(), calls=%async_computation.18 | async-start | bytes 147456 | tf_op jit(solution)/shard_map/reduce_scatter | solution.py:300
  736.5 102.0 %reduce-scatter.26.cloned.1.call-start = ((), (), s32[]{:S(2)}) async-start(), calls=%async_computation.19 | async-start | bytes 147456 | tf_op jit(solution)/shard_map/reduce_scatter | solution.py:303
  739.4 135.6 %reduce-scatter.22.cloned.1.call-start = ((), (), s32[]{:S(2)}) async-start(), calls=%async_computation.17 | async-start | bytes 147456 | tf_op jit(solution)/shard_map/reduce_scatter | solution.py:297
  742.5 195.1 %reduce-scatter.20.cloned.1.call-start = ((), (), s32[]{:S(2)}) async-start(), calls=%async_computation.16 | async-start | bytes 3932160 | tf_op jit(solution)/shard_map/reduce_scatter | solution.py:266
  747.7 189.9 %copy-start.8 = (bf16[768,512]{1,0:T(8,128)(2,1)S(1)}, bf16[768,512]{1,0:T(8,128)(2,1)}, u32[]{:S(2)}) copy-start(bf16[768,512]{1,0:T(8,128)(2,1)} %param.28) | copy-start | bytes 2359300
  747.7 189.9 %copy-start.47 = (f32[768]{0:T(1024)S(1)}, f32[768]{0:T(1024)}, u32[]{:S(2)}) copy-start(f32[768]{0:T(1024)} %copy-done.46) | copy-start | bytes 9220
  747.7 189.9 %copy-start.54 = (f32[512]{0:T(512)S(1)}, f32[512]{0:T(512)}, u32[]{:S(2)}) copy-start(f32[512]{0:T(512)} %copy-done.53) | copy-start | bytes 6148
  747.7 191.6 %copy-start.56 = (f32[768]{0:T(1024)S(1)}, f32[768]{0:T(1024)}, u32[]{:S(2)}) copy-start(f32[768]{0:T(1024)} %copy-done.55) | copy-start | bytes 9220
  747.7 191.6 %copy-start.52 = (f32[768]{0:T(1024)S(1)}, f32[768]{0:T(1024)}, u32[]{:S(2)}) copy-start(f32[768]{0:T(1024)} %copy-done.51) | copy-start | bytes 9220
  752.5 187.9 %copy-start.65 = (f32[512]{0:T(512)S(1)}, f32[512]{0:T(512)}, u32[]{:S(2)}) copy-start(f32[512]{0:T(512)} %get-tuple-element.338) | copy-start | bytes 6148
  752.5 187.9 %copy-start.66 = (f32[512]{0:T(512)S(1)}, f32[512]{0:T(512)}, u32[]{:S(2)}) copy-start(f32[512]{0:T(512)} %get-tuple-element.439) | copy-start | bytes 6148
  752.5 187.9 %copy-start.67 = (f32[512]{0:T(512)S(1)}, f32[512]{0:T(512)}, u32[]{:S(2)}) copy-start(f32[512]{0:T(512)} %get-tuple-element.343) | copy-start | bytes 6148
  752.5 233.3 %copy-start.17 = (f32[768,512]{1,0:T(8,128)S(1)}, f32[768,512]{1,0:T(8,128)}, u32[]{:S(2)}) copy-start(f32[768,512]{1,0:T(8,128)} %copy-done.16) | copy-start | bytes 4718596
  (127 other events, 1337.1 us)
Sparse Core Ops, SparseCore 0:
  35.8 62.8 all-gather.5
  174.1 58.8 reduce-scatter.13
  347.1 62.1 reduce-scatter.15
  414.2 63.5 all-gather.7
  491.9 58.8 reduce-scatter.17
  560.3 63.5 all-gather.9
  627.0 32.7 reduce-scatter.31
  663.2 34.1 reduce-scatter.29
  733.4 32.0 reduce-scatter.27
  768.6 33.3 reduce-scatter.23
  805.1 33.3 reduce-scatter.25
  841.6 33.3 reduce-scatter.21
  877.3 60.2 reduce-scatter.19
